TPU v7x, 256 devices: a whole 4x4x8 slice. The times are simulated.
256 devices in a mesh: chan: 8 (over x_lo, y), lon: 32 (over x_hi, z, core).
Axes of the slice: x: 4 (x_hi: 2, x_lo: 2; x = x_hi * 2 + x_lo), y: 4, z: 8, core: 2. Of those that a mesh axis runs over, the one named last changes fastest.
Arguments:
- symbols: int32 [320, 4, 128, 128], P('chan', None, 'lon'), may hold values from -3 to 3
- hyper_mean: bfloat16 [320, 4, 128, 128], P('chan', None, 'lon'), may hold values from -6 to 6
- slice_order: int32 [8], replicated, may hold values from 0 to 7, each once
- hyper_weight: bfloat16 [8, 15, 224, 40], P('chan'), may hold values from -0.25 to 0.25
- ctx_weight: bfloat16 [8, 15, 224, 320], P('chan'), may hold values from -0.09375 to 0.09375
- ctx_bias: float32 [8, 224], P('chan'), may hold values from -6 to 6
- out_weight: bfloat16 [8, 40, 224], P('chan'), may hold values from -0.375 to 0.375
- gdn_beta: float32 [320], replicated, may hold values from 0.5 to 4
- gdn_gamma: float32 [320, 320], replicated, may hold values from 0 to 0.006
- tconv_weight: bfloat16 [27, 64, 320], P(None, 'chan'), may hold values from -0.078125 to 0.078125
Outputs:
- upsampled: bfloat16 [64, 8, 256, 256], P('chan', None, 'lon')
Inputs may be any that keep to these rules, and one draw needn't show every extreme that they name: `slice_order`: each slice number appears exactly once.
All inputs are finite; a program needn't handle non-finite values.
Results may differ from a plain program's by a relative error of at most 0.014.
Values may be sent and summed in bfloat16 or wider, within the bound.
No kernel may reach another device: no remote copies, remote signals or barrier semaphores. Data moves between devices by JAX's collectives and lax.ppermute only.
A program may use at most 64 MiB of HBM per device.

v0:
```python
import jax
import jax.numpy as jnp
from jax import lax
from jax.sharding import PartitionSpec as P


def with_halo(value, sides, width):
    for axis, dim in sides:
        size, length = (lax.axis_size(axis), value.shape[dim])
        up = [(i, (i + 1) % size) for i in range(size)]
        down = [(j, i) for i, j in up]
        last = lax.slice_in_dim(value, length - width, length, axis=dim)
        first = lax.slice_in_dim(value, 0, width, axis=dim)
        before = lax.ppermute(last, axis, up)
        after = lax.ppermute(first, axis, down)
        value = jnp.concatenate([before, value, after], axis=dim)
    return value


def broadcast(block, axis, owner):
    block = jnp.where(lax.axis_index(axis) == owner, block, jnp.zeros_like(block))
    return lax.psum(block, axis)


def from_behind(value, axis, steps):
    count = lax.axis_size(axis)
    pairs = [(source, (source + steps) % count) for source in range(count)]
    return lax.ppermute(value, axis, pairs)


def band_conv(wide_band, weight):
    lon_len = wide_band.shape[2] - 4
    lat_len = wide_band.shape[3]
    padded = jnp.pad(wide_band, ((0, 0), (0, 0), (0, 0), (1, 1)))
    summed = jnp.zeros((weight.shape[1], wide_band.shape[1], lon_len, lat_len), jnp.float32)
    for shift_lon in range(5):
        for shift_lat in range(3):
            section = padded[:, :, shift_lon : shift_lon + lon_len, shift_lat : shift_lat + lat_len]
            summed = summed + jnp.einsum(
                "hc,cvxt->hvxt",
                weight[shift_lon * 3 + shift_lat],
                section,
                preferred_element_type=jnp.float32,
            )
    return summed


def upsample(extended, weight):
    lev_len = extended.shape[1] - 1
    lon_len = extended.shape[2] - 1
    lat_len = extended.shape[3] - 1
    tap_table = (((1, 0),), ((2, 0), (0, 1)))
    parity_parts = []
    for par_lev in range(2):
        for par_lon in range(2):
            for par_lat in range(2):
                summed = jnp.zeros((weight.shape[1], lev_len, lon_len, lat_len), jnp.float32)
                for tap_lev, off_lev in tap_table[par_lev]:
                    for tap_lon, off_lon in tap_table[par_lon]:
                        for tap_lat, off_lat in tap_table[par_lat]:
                            section = extended[
                                :,
                                off_lev : off_lev + lev_len,
                                off_lon : off_lon + lon_len,
                                off_lat : off_lat + lat_len,
                            ]
                            tap_weight = weight[tap_lev * 9 + tap_lon * 3 + tap_lat]
                            summed = summed + jnp.einsum(
                                "oc,cvxt->ovxt",
                                tap_weight,
                                section,
                                preferred_element_type=jnp.float32,
                            )
                parity_parts.append(summed)
    stacked = jnp.stack(parity_parts).reshape((2, 2, 2) + parity_parts[0].shape)
    reordered = jnp.transpose(stacked, (3, 4, 0, 5, 1, 6, 2))
    return reordered.reshape(weight.shape[1], 2 * lev_len, 2 * lon_len, 2 * lat_len)


def pad_ends(extended):
    return jnp.pad(extended, ((0, 0), (0, 1), (0, 0), (0, 1)))


def normalize(rows_in, values, gamma_rows, beta_rows):
    squares = values.astype(jnp.float32) * values.astype(jnp.float32)
    energy = beta_rows[:, None, None, None] + jnp.einsum(
        "ij,jvxt->ivxt", gamma_rows, squares, precision=lax.Precision.HIGHEST
    )
    return (rows_in.astype(jnp.float32) * jnp.sqrt(energy)).astype(jnp.bfloat16)


def local(
    symbols,
    hyper_mean,
    slice_order,
    hyper_weight,
    ctx_weight,
    ctx_bias,
    out_weight,
    gdn_beta,
    gdn_gamma,
    tconv_weight,
):
    slice_width, levels, lon_len, lat_len = symbols.shape
    channels = ctx_weight.shape[3]
    hyper_wide = with_halo(hyper_mean, (("lon", 2),), 2)
    start_pre = band_conv(hyper_wide, hyper_weight[0]) + ctx_bias[0][:, None, None, None]
    symbol_values = symbols.astype(jnp.float32)
    decoded = jnp.zeros((channels, levels, lon_len, lat_len), jnp.bfloat16)
    column = jnp.zeros((channels, levels, 1, lat_len), jnp.bfloat16)

    def decode(step_id, carry):
        pre_act, decoded, column = carry
        slice_id = slice_order[step_id]
        first_row = slice_id * slice_width
        hidden = jax.nn.gelu(pre_act, approximate=False).astype(jnp.bfloat16)
        slice_mean = jnp.einsum(
            "ch,hvxt->cvxt", out_weight[0], hidden, preferred_element_type=jnp.float32
        )
        candidate = (symbol_values + slice_mean).astype(jnp.bfloat16)
        decoded_rows = broadcast(candidate, "chan", slice_id)
        wide_band = with_halo(decoded_rows, (("lon", 2),), 2)
        weight_block = lax.dynamic_slice_in_dim(ctx_weight[0], first_row, slice_width, 2)
        pre_act = pre_act + band_conv(wide_band, weight_block)
        decoded = lax.dynamic_update_slice_in_dim(decoded, decoded_rows, first_row, 0)
        column = lax.dynamic_update_slice_in_dim(
            column, wide_band[:, :, lon_len + 2 : lon_len + 3], first_row, 0
        )
        return (pre_act, decoded, column)

    pre_act, decoded, column = lax.fori_loop(
        0, lax.axis_size("chan"), decode, (start_pre, decoded, column)
    )
    normed = normalize(decoded, decoded, gdn_gamma, gdn_beta)
    next_column = from_behind(normed[:, :, :1], "lon", -1)
    extended = jnp.concatenate([normed, next_column], axis=2)
    result = upsample(pad_ends(extended), tconv_weight)
    return result.astype(jnp.bfloat16)


def solution(mesh):
    placed = (
        P("chan", None, "lon", None),
        P("chan", None, "lon", None),
        P(),
        P("chan", None, None, None),
        P("chan", None, None, None),
        P("chan", None),
        P("chan", None, None),
        P(),
        P(),
        P(None, "chan", None),
    )
    return jax.shard_map(
        local, mesh=mesh, in_specs=placed, out_specs=P("chan", None, "lon", None), check_vma=False
    )
```

profile of v0, /device:TPU:225, one launch (start us, length us, event | category | flops | bytes accessed | tf_op | source)
XLA Modules:
  0.0 967.9 jit_solution(5462443687672508898)
XLA Ops:
  8.5 1.4 fusion.175
  10.0 5.3 collective-permute-done.3
  21.7 3.3 fusion.99
  25.0 1.3 broadcast_in_dim.4
  26.3 896.5 %while.17 = (s32[]{:T(128)}, f32[224,4,4,128]{3,0,2,1:T(8,128)}, bf16[320,4,4,128]{3,0,2,1:T(8,128)(2,1)}, s32[8]{0:T(128)S(1)}, bf16[1,15,224,320]{2,3,1,0:T(8,...) while((s32[]{:T(128)}, f32[224,4,4,128]{3,0,2,1:T(8,128)}, ...), condition=%wide.region_2.3_spmd, body=%wide.region_0.2_spmd.sunk | while | flops 626227200 | bytes 64425220 | solution.py:131
  27.5 6.2 fusion.339
  34.3 70.3 %all-reduce.5.cloned.1.call-done = bf16[40,4,4,128]{3,0,2,1:T(8,128)(2,1)} async-done(((bf16[40,4,4,128]{3,0,2,1:T(8,128)(2,1)}), bf16[40,4,4,128]{3,0,2,1:T(8,128)(2,1)}) %all-reduce.5.cloned.1.call-update) | async-done | bytes 163856 | tf_op jit(solution)/shard_map/while/body/eval_jaxpr/psum | solution.py:22
  105.6 7.2 collective-permute-start
  112.9 1.3 fusion.348
  115.1 5.2 collective-permute-done.1
  128.8 1.2 fusion.350
  133.5 1.2 fusion.344
  135.9 4.6 add_add_fusion.2
  141.7 6.2 fusion.339
  148.5 67.9 %all-reduce.5.cloned.1.call-done = bf16[40,4,4,128]{3,0,2,1:T(8,128)(2,1)} async-done(((bf16[40,4,4,128]{3,0,2,1:T(8,128)(2,1)}), bf16[40,4,4,128]{3,0,2,1:T(8,128)(2,1)}) %all-reduce.5.cloned.1.call-update) | async-done | bytes 163856 | tf_op jit(solution)/shard_map/while/body/eval_jaxpr/psum | solution.py:22
  217.4 7.2 collective-permute-start
  224.6 1.3 fusion.348
  226.9 5.2 collective-permute-done.1
  240.5 1.2 fusion.350
  245.3 1.2 fusion.344
  247.6 4.6 add_add_fusion.2
  253.4 6.2 fusion.339
  260.2 67.9 %all-reduce.5.cloned.1.call-done = bf16[40,4,4,128]{3,0,2,1:T(8,128)(2,1)} async-done(((bf16[40,4,4,128]{3,0,2,1:T(8,128)(2,1)}), bf16[40,4,4,128]{3,0,2,1:T(8,128)(2,1)}) %all-reduce.5.cloned.1.call-update) | async-done | bytes 163856 | tf_op jit(solution)/shard_map/while/body/eval_jaxpr/psum | solution.py:22
  329.1 7.2 collective-permute-start
  336.3 1.3 fusion.348
  338.6 5.2 collective-permute-done.1
  352.2 1.2 fusion.350
  359.3 4.6 add_add_fusion.2
  365.1 6.2 fusion.339
  371.9 67.9 %all-reduce.5.cloned.1.call-done = bf16[40,4,4,128]{3,0,2,1:T(8,128)(2,1)} async-done(((bf16[40,4,4,128]{3,0,2,1:T(8,128)(2,1)}), bf16[40,4,4,128]{3,0,2,1:T(8,128)(2,1)}) %all-reduce.5.cloned.1.call-update) | async-done | bytes 163856 | tf_op jit(solution)/shard_map/while/body/eval_jaxpr/psum | solution.py:22
  440.8 7.2 collective-permute-start
  448.1 1.4 fusion.348
  450.3 5.2 collective-permute-done.1
  471.1 4.6 add_add_fusion.2
  476.8 6.2 fusion.339
  483.7 68.0 %all-reduce.5.cloned.1.call-done = bf16[40,4,4,128]{3,0,2,1:T(8,128)(2,1)} async-done(((bf16[40,4,4,128]{3,0,2,1:T(8,128)(2,1)}), bf16[40,4,4,128]{3,0,2,1:T(8,128)(2,1)}) %all-reduce.5.cloned.1.call-update) | async-done | bytes 163856 | tf_op jit(solution)/shard_map/while/body/eval_jaxpr/psum | solution.py:22
  552.7 7.2 collective-permute-start
  559.9 1.3 fusion.348
  562.2 5.2 collective-permute-done.1
  582.9 4.6 add_add_fusion.2
  588.7 6.2 fusion.339
  595.5 67.9 %all-reduce.5.cloned.1.call-done = bf16[40,4,4,128]{3,0,2,1:T(8,128)(2,1)} async-done(((bf16[40,4,4,128]{3,0,2,1:T(8,128)(2,1)}), bf16[40,4,4,128]{3,0,2,1:T(8,128)(2,1)}) %all-reduce.5.cloned.1.call-update) | async-done | bytes 163856 | tf_op jit(solution)/shard_map/while/body/eval_jaxpr/psum | solution.py:22
  664.4 7.2 collective-permute-start
  671.6 1.3 fusion.348
  673.9 5.2 collective-permute-done.1
  692.2 1.2 fusion.344
  694.6 4.6 add_add_fusion.2
  700.4 6.2 fusion.339
  707.2 67.9 %all-reduce.5.cloned.1.call-done = bf16[40,4,4,128]{3,0,2,1:T(8,128)(2,1)} async-done(((bf16[40,4,4,128]{3,0,2,1:T(8,128)(2,1)}), bf16[40,4,4,128]{3,0,2,1:T(8,128)(2,1)}) %all-reduce.5.cloned.1.call-update) | async-done | bytes 163856 | tf_op jit(solution)/shard_map/while/body/eval_jaxpr/psum | solution.py:22
  776.1 7.2 collective-permute-start
  783.3 1.4 fusion.348
  785.6 5.2 collective-permute-done.1
  799.3 1.2 fusion.350
  806.3 4.6 add_add_fusion.2
  812.1 6.2 fusion.339
  819.0 67.9 %all-reduce.5.cloned.1.call-done = bf16[40,4,4,128]{3,0,2,1:T(8,128)(2,1)} async-done(((bf16[40,4,4,128]{3,0,2,1:T(8,128)(2,1)}), bf16[40,4,4,128]{3,0,2,1:T(8,128)(2,1)}) %all-reduce.5.cloned.1.call-update) | async-done | bytes 163856 | tf_op jit(solution)/shard_map/while/body/eval_jaxpr/psum | solution.py:22
  887.9 7.2 collective-permute-start
  895.1 1.3 fusion.348
  897.3 5.2 collective-permute-done.1
  918.1 4.6 add_add_fusion.2
  922.7 7.1 fusion.98
  932.5 9.5 collective-permute-done.4
  949.4 7.2 copy.26
  956.6 4.4 copy.27
  (264 shorter events, 153.6 us)
Async XLA Ops:
  6.5 916.2 %copy-start = (f32[320,320]{1,0:T(8,128)S(1)}, f32[320,320]{1,0:T(8,128)}, u32[]{:S(2)}) copy-start(f32[320,320]{1,0:T(8,128)} %param.20) | copy-start | bytes 1228804
  6.5 3.3 copy-start.3
  7.6 8.0 copy-start.4
  7.6 2.3 collective-permute-start.2
  7.8 7.5 collective-permute-start.3
  18.8 0.9 copy-start.2
  20.8 0.9 copy-start.6
  21.7 4.6 copy-start.7
  21.7 4.6 copy-start.9
  26.3 896.5 %copy-start.8 = (f32[320]{0:T(512)S(1)}, f32[320]{0:T(512)}, u32[]{:S(2)}) copy-start(f32[320]{0:T(512)} %param.19) | copy-start | bytes 3844
  26.3 78.4 %all-reduce.5.cloned.1.call-start = ((), (), s32[]{:S(2)}) async-start(), calls=%async_computation | async-start | bytes 327680 | tf_op jit(solution)/shard_map/while/body/eval_jaxpr/psum | solution.py:22
  104.7 9.7 %copy-start.1 = (bf16[40,4,4,128]{3,0,2,1:T(8,128)(2,1)S(1)}, bf16[40,4,4,128]{3,0,2,1:T(8,128)(2,1)}, u32[]{:S(2)}) copy-start(bf16[40,4,4,128]{3,0,2,1:T(8,128)(2,1)} %all-reduce.5.cloned.1.call-done) | copy-start | bytes 491524 | tf_op jit(solution)/shard_map/while
  105.6 8.7 collective-permute-start
  112.9 7.5 collective-permute-start.1
  140.5 75.9 %all-reduce.5.cloned.1.call-start = ((), (), s32[]{:S(2)}) async-start(), calls=%async_computation | async-start | bytes 327680 | tf_op jit(solution)/shard_map/while/body/eval_jaxpr/psum | solution.py:22
  216.4 9.7 %copy-start.1 = (bf16[40,4,4,128]{3,0,2,1:T(8,128)(2,1)S(1)}, bf16[40,4,4,128]{3,0,2,1:T(8,128)(2,1)}, u32[]{:S(2)}) copy-start(bf16[40,4,4,128]{3,0,2,1:T(8,128)(2,1)} %all-reduce.5.cloned.1.call-done) | copy-start | bytes 491524 | tf_op jit(solution)/shard_map/while
  217.4 8.7 collective-permute-start
  224.6 7.5 collective-permute-start.1
  252.3 75.8 %all-reduce.5.cloned.1.call-start = ((), (), s32[]{:S(2)}) async-start(), calls=%async_computation | async-start | bytes 327680 | tf_op jit(solution)/shard_map/while/body/eval_jaxpr/psum | solution.py:22
  328.1 9.7 %copy-start.1 = (bf16[40,4,4,128]{3,0,2,1:T(8,128)(2,1)S(1)}, bf16[40,4,4,128]{3,0,2,1:T(8,128)(2,1)}, u32[]{:S(2)}) copy-start(bf16[40,4,4,128]{3,0,2,1:T(8,128)(2,1)} %all-reduce.5.cloned.1.call-done) | copy-start | bytes 491524 | tf_op jit(solution)/shard_map/while
  329.1 8.7 collective-permute-start
  336.3 7.5 collective-permute-start.1
  363.9 75.9 %all-reduce.5.cloned.1.call-start = ((), (), s32[]{:S(2)}) async-start(), calls=%async_computation | async-start | bytes 327680 | tf_op jit(solution)/shard_map/while/body/eval_jaxpr/psum | solution.py:22
  439.9 9.7 %copy-start.1 = (bf16[40,4,4,128]{3,0,2,1:T(8,128)(2,1)S(1)}, bf16[40,4,4,128]{3,0,2,1:T(8,128)(2,1)}, u32[]{:S(2)}) copy-start(bf16[40,4,4,128]{3,0,2,1:T(8,128)(2,1)} %all-reduce.5.cloned.1.call-done) | copy-start | bytes 491524 | tf_op jit(solution)/shard_map/while
  440.8 8.7 collective-permute-start
  448.0 7.5 collective-permute-start.1
  475.7 76.0 %all-reduce.5.cloned.1.call-start = ((), (), s32[]{:S(2)}) async-start(), calls=%async_computation | async-start | bytes 327680 | tf_op jit(solution)/shard_map/while/body/eval_jaxpr/psum | solution.py:22
  551.7 9.7 %copy-start.1 = (bf16[40,4,4,128]{3,0,2,1:T(8,128)(2,1)S(1)}, bf16[40,4,4,128]{3,0,2,1:T(8,128)(2,1)}, u32[]{:S(2)}) copy-start(bf16[40,4,4,128]{3,0,2,1:T(8,128)(2,1)} %all-reduce.5.cloned.1.call-done) | copy-start | bytes 491524 | tf_op jit(solution)/shard_map/while
  552.7 8.7 collective-permute-start
  559.9 7.5 collective-permute-start.1
  587.5 75.9 %all-reduce.5.cloned.1.call-start = ((), (), s32[]{:S(2)}) async-start(), calls=%async_computation | async-start | bytes 327680 | tf_op jit(solution)/shard_map/while/body/eval_jaxpr/psum | solution.py:22
  663.4 9.7 %copy-start.1 = (bf16[40,4,4,128]{3,0,2,1:T(8,128)(2,1)S(1)}, bf16[40,4,4,128]{3,0,2,1:T(8,128)(2,1)}, u32[]{:S(2)}) copy-start(bf16[40,4,4,128]{3,0,2,1:T(8,128)(2,1)} %all-reduce.5.cloned.1.call-done) | copy-start | bytes 491524 | tf_op jit(solution)/shard_map/while
  664.4 8.7 collective-permute-start
  671.6 7.5 collective-permute-start.1
  699.2 75.9 %all-reduce.5.cloned.1.call-start = ((), (), s32[]{:S(2)}) async-start(), calls=%async_computation | async-start | bytes 327680 | tf_op jit(solution)/shard_map/while/body/eval_jaxpr/psum | solution.py:22
  775.1 9.7 %copy-start.1 = (bf16[40,4,4,128]{3,0,2,1:T(8,128)(2,1)S(1)}, bf16[40,4,4,128]{3,0,2,1:T(8,128)(2,1)}, u32[]{:S(2)}) copy-start(bf16[40,4,4,128]{3,0,2,1:T(8,128)(2,1)} %all-reduce.5.cloned.1.call-done) | copy-start | bytes 491524 | tf_op jit(solution)/shard_map/while
  776.1 8.7 collective-permute-start
  783.3 7.5 collective-permute-start.1
  811.0 75.9 %all-reduce.5.cloned.1.call-start = ((), (), s32[]{:S(2)}) async-start(), calls=%async_computation | async-start | bytes 327680 | tf_op jit(solution)/shard_map/while/body/eval_jaxpr/psum | solution.py:22
  886.9 9.7 %copy-start.1 = (bf16[40,4,4,128]{3,0,2,1:T(8,128)(2,1)S(1)}, bf16[40,4,4,128]{3,0,2,1:T(8,128)(2,1)}, u32[]{:S(2)}) copy-start(bf16[40,4,4,128]{3,0,2,1:T(8,128)(2,1)} %all-reduce.5.cloned.1.call-done) | copy-start | bytes 491524 | tf_op jit(solution)/shard_map/while
  887.9 8.7 collective-permute-start
  895.1 7.5 collective-permute-start.1
  922.7 7.1 copy-start.5
  931.6 10.5 %collective-permute-start.4 = (bf16[320,4,1,128]{3,0,2,1:T(8,128)(2,1)S(1)}, bf16[320,4,1,128]{3,0,2,1:T(8,128)(2,1)S(1)}, u32[]{:S(2)}, u32[]{:S(2)}) collective-permute-start(bf16[320,4,1,128]{3,0,2,1:T(8,128)(2,1)S(1)} %slice.676), channel_id=1, source_target_pairs={{0,31},{1,0},{2,1},{3,2},{4,3},{5,4},{6,5},{7,6},{8,7},{9,8},{10,9... | collective-permute-start | bytes 983048 | tf_op jit(solution)/shard_map/ppermute | solution.py:28
Sparse Core Ops, SparseCore 0:
  33.9 70.7 all-reduce.4
  148.0 68.3 all-reduce.4
  259.8 68.2 all-reduce.4
  371.5 68.3 all-reduce.4
  483.2 68.3 all-reduce.4
  595.1 68.2 all-reduce.4
  706.8 68.3 all-reduce.4
  818.5 68.2 all-reduce.4
where the time goes:
time: 975 us; the launch traced here: 968 us
  waiting for transfers between devices  603 us (62%)
  matrix products  246 us (25%)
  starting transfers between devices  58.9 us (6%)
  local copies, waits for them, and re-layouts  33.1 us (3%)
  between operations  13.7 us (1%)
    psum x8, waiting for transfers between devices, broadcast(): return lax.psum(block, axis)  546 us
    dot_general x135, matrix products, band_conv(): jnp.einsum('hc,cvxt->hvxt', weight[shift_lon * 3 + shift_lat], section, p...  180 us
    ppermute x9, starting transfers between devices, with_halo(): before = lax.ppermute(last, axis, up)  57.8 us
    dot_general x8, matrix products, decode(): jnp.einsum('ch,hvxt->cvxt', out_weight[0], hidden, preferred_element_type...  50 us
    ppermute x9, waiting for transfers between devices, with_halo(): after = lax.ppermute(first, axis, down)  47 us
  transfers between devices with their start and end apart: 27, of which 26 were waited for; matrix products, arithmetic and copies ran while one was open for 2% of the time, Pallas kernels for 0%

commit v1 on v0

--- a/solution.py
+++ b/solution.py
@@ -19,7 +19,7 @@
 
 def broadcast(block, axis, owner):
     block = jnp.where(lax.axis_index(axis) == owner, block, jnp.zeros_like(block))
-    return lax.psum(block, axis)
+    return jnp.sum(lax.all_gather(block, axis), axis=0)
 
 
 def from_behind(value, axis, steps):

time: 975 us -> 699 us (0.72)
  waiting for transfers between devices: 603 us -> 303 us
  matrix products: 246 us -> 258 us
  other arithmetic: 3.04 us -> 15 us
    psum x8 -> x0, waiting for transfers between devices: 546 us -> none  [broadcast(): return lax.psum(block, axis)]
    all_gather x0 -> x8, waiting for transfers between devices: none -> 287 us  [broadcast(): return jnp.sum(lax.all_gather(block, axis), axis=0)]
    ppermute x9, starting transfers between devices: 0.67 us -> 51.4 us  [with_halo(): after = lax.ppermute(first, axis, down)]
    ppermute x9, starting transfers between devices: 57.8 us -> 14.1 us  [with_halo(): before = lax.ppermute(last, axis, up)]
    ppermute x9, waiting for transfers between devices: 47 us -> 6.53 us  [with_halo(): after = lax.ppermute(first, axis, down)]
    reduce_sum x0 -> x8, other arithmetic: none -> 12 us  [broadcast(): return jnp.sum(lax.all_gather(block, axis), axis=0)]
    dot_general x135, matrix products: 180 us -> 191 us  [band_conv(): jnp.einsum('hc,cvxt->hvxt', weight[shift_lon * 3 + shift_lat], section, p...]
  transfers between devices with their start and end apart: 27 -> 27, of which waited for: 26 -> 18; matrix products, arithmetic and copies ran while one was open for 2% -> 2% of each run, Pallas kernels for 0% -> 0%
where the time goes in v1:
time: 699 us; the launch traced here: 692 us
  waiting for transfers between devices  303 us (43%)
  matrix products  258 us (37%)
  starting transfers between devices  66.1 us (9%)
  local copies, waits for them, and re-layouts  25.4 us (4%)
  other arithmetic  15 us (2%)
  between operations  13.7 us (2%)
  loops' own time  10.8 us (2%)
    all_gather x8, waiting for transfers between devices, broadcast(): return jnp.sum(lax.all_gather(block, axis), axis=0)  287 us
    dot_general x135, matrix products, band_conv(): jnp.einsum('hc,cvxt->hvxt', weight[shift_lon * 3 + shift_lat], section, p...  191 us
    ppermute x9, starting transfers between devices, with_halo(): after = lax.ppermute(first, axis, down)  51.4 us
    dot_general x8, matrix products, decode(): jnp.einsum('ch,hvxt->cvxt', out_weight[0], hidden, preferred_element_type...  50 us
    ppermute x9, starting transfers between devices, with_halo(): before = lax.ppermute(last, axis, up)  14.1 us
  transfers between devices with their start and end apart: 27, of which 18 were waited for; matrix products, arithmetic and copies ran while one was open for 2% of the time, Pallas kernels for 0%

profile of v1, /device:TPU:225, one launch (start us, length us, event | category | flops | bytes accessed | tf_op | source)
XLA Modules:
  0.0 691.9 jit_solution(3239844957052482611)
XLA Ops:
  8.5 1.4 fusion.181
  10.0 5.3 collective-permute-done.3
  21.7 3.3 fusion.105
  26.3 620.4 %while.18 = (s32[]{:T(128)}, f32[224,4,4,128]{3,0,2,1:T(8,128)}, bf16[320,4,4,128]{3,0,2,1:T(8,128)(2,1)}, s32[8]{0:T(128)S(1)}, bf16[1,15,224,320]{2,3,1,0:T(8,...) while((s32[]{:T(128)}, f32[224,4,4,128]{3,0,2,1:T(8,128)}, ...), condition=%wide.region_2.3_spmd, body=%wide.region_0.2_spmd.sunk | while | flops 628029440 | bytes 68357352 | solution.py:131
  27.7 6.2 fusion.341
  34.6 34.7 %all-gather.5.cloned.1.call-done = bf16[320,4,4,128]{3,0,2,1:T(8,128)(2,1)} async-done(((bf16[40,4,4,128]{3,0,2,1:T(8,128)(2,1)}), bf16[320,4,4,128]{3,0,2,1:T(8,128)(2,1)}) %all-gather.5.cloned.1.call-update) | async-done | bytes 1310736 | tf_op jit(solution)/shard_map/while/body/eval_jaxpr/all_gather | solution.py:22
  69.3 1.5 reduce_sum.15
  70.8 6.4 collective-permute-start
  77.2 1.7 collective-permute-start.1
  95.3 2.4 fusion.343
  97.7 5.1 add_add_fusion.2
  104.1 6.2 fusion.341
  111.0 36.0 %all-gather.5.cloned.1.call-done = bf16[320,4,4,128]{3,0,2,1:T(8,128)(2,1)} async-done(((bf16[40,4,4,128]{3,0,2,1:T(8,128)(2,1)}), bf16[320,4,4,128]{3,0,2,1:T(8,128)(2,1)}) %all-gather.5.cloned.1.call-update) | async-done | bytes 1310736 | tf_op jit(solution)/shard_map/while/body/eval_jaxpr/all_gather | solution.py:22
  147.0 1.5 reduce_sum.15
  148.5 6.4 collective-permute-start
  154.9 1.7 collective-permute-start.1
  173.0 2.4 fusion.343
  175.4 5.1 add_add_fusion.2
  181.8 6.2 fusion.341
  188.7 36.0 %all-gather.5.cloned.1.call-done = bf16[320,4,4,128]{3,0,2,1:T(8,128)(2,1)} async-done(((bf16[40,4,4,128]{3,0,2,1:T(8,128)(2,1)}), bf16[320,4,4,128]{3,0,2,1:T(8,128)(2,1)}) %all-gather.5.cloned.1.call-update) | async-done | bytes 1310736 | tf_op jit(solution)/shard_map/while/body/eval_jaxpr/all_gather | solution.py:22
  224.7 1.5 reduce_sum.15
  226.2 6.4 collective-permute-start
  232.6 1.7 collective-permute-start.1
  250.7 2.4 fusion.343
  253.1 5.1 add_add_fusion.2
  259.5 6.2 fusion.341
  266.4 36.0 %all-gather.5.cloned.1.call-done = bf16[320,4,4,128]{3,0,2,1:T(8,128)(2,1)} async-done(((bf16[40,4,4,128]{3,0,2,1:T(8,128)(2,1)}), bf16[320,4,4,128]{3,0,2,1:T(8,128)(2,1)}) %all-gather.5.cloned.1.call-update) | async-done | bytes 1310736 | tf_op jit(solution)/shard_map/while/body/eval_jaxpr/all_gather | solution.py:22
  302.4 1.5 reduce_sum.15
  303.9 6.4 collective-permute-start
  310.3 1.7 collective-permute-start.1
  328.4 2.4 fusion.343
  330.8 5.1 add_add_fusion.2
  337.2 6.2 fusion.341
  344.1 36.0 %all-gather.5.cloned.1.call-done = bf16[320,4,4,128]{3,0,2,1:T(8,128)(2,1)} async-done(((bf16[40,4,4,128]{3,0,2,1:T(8,128)(2,1)}), bf16[320,4,4,128]{3,0,2,1:T(8,128)(2,1)}) %all-gather.5.cloned.1.call-update) | async-done | bytes 1310736 | tf_op jit(solution)/shard_map/while/body/eval_jaxpr/all_gather | solution.py:22
  380.1 1.5 reduce_sum.15
  381.6 6.4 collective-permute-start
  388.0 1.7 collective-permute-start.1
  406.1 2.4 fusion.343
  408.5 5.1 add_add_fusion.2
  414.9 6.2 fusion.341
  421.8 36.0 %all-gather.5.cloned.1.call-done = bf16[320,4,4,128]{3,0,2,1:T(8,128)(2,1)} async-done(((bf16[40,4,4,128]{3,0,2,1:T(8,128)(2,1)}), bf16[320,4,4,128]{3,0,2,1:T(8,128)(2,1)}) %all-gather.5.cloned.1.call-update) | async-done | bytes 1310736 | tf_op jit(solution)/shard_map/while/body/eval_jaxpr/all_gather | solution.py:22
  457.8 1.5 reduce_sum.15
  459.3 6.4 collective-permute-start
  465.7 1.7 collective-permute-start.1
  483.8 2.4 fusion.343
  486.2 5.1 add_add_fusion.2
  492.6 6.2 fusion.341
  499.5 36.0 %all-gather.5.cloned.1.call-done = bf16[320,4,4,128]{3,0,2,1:T(8,128)(2,1)} async-done(((bf16[40,4,4,128]{3,0,2,1:T(8,128)(2,1)}), bf16[320,4,4,128]{3,0,2,1:T(8,128)(2,1)}) %all-gather.5.cloned.1.call-update) | async-done | bytes 1310736 | tf_op jit(solution)/shard_map/while/body/eval_jaxpr/all_gather | solution.py:22
  535.5 1.5 reduce_sum.15
  537.0 6.4 collective-permute-start
  543.4 1.7 collective-permute-start.1
  561.5 2.4 fusion.343
  563.9 5.1 add_add_fusion.2
  570.3 6.2 fusion.341
  577.2 36.0 %all-gather.5.cloned.1.call-done = bf16[320,4,4,128]{3,0,2,1:T(8,128)(2,1)} async-done(((bf16[40,4,4,128]{3,0,2,1:T(8,128)(2,1)}), bf16[320,4,4,128]{3,0,2,1:T(8,128)(2,1)}) %all-gather.5.cloned.1.call-update) | async-done | bytes 1310736 | tf_op jit(solution)/shard_map/while/body/eval_jaxpr/all_gather | solution.py:22
  613.2 1.5 reduce_sum.15
  614.7 6.4 collective-permute-start
  621.1 1.7 collective-permute-start.1
  639.2 2.4 fusion.343
  641.6 5.1 add_add_fusion.2
  646.7 7.1 %fusion.104 = bf16[320,4,4,128]{3,0,2,1:T(8,128)(2,1)S(1)} fusion(bf16[320,4,4,128]{3,0,2,1:T(8,128)(2,1)} %get-tuple-element.201, f32[320]{0:T(512)S(1)} %copy-done.7, f32[320,320]{1,0:T(8,128)S(1)} %copy-done), kind=kOutput, calls=%fused_computation.142 | convolution fusion | flops 2520514560 | bytes 3032320 | tf_op jit(solution)/shard_map/ij,jvxt->ivxt/dot_general | solution.py:86
  656.6 9.5 %collective-permute-done.4 = bf16[320,4,1,128]{3,0,2,1:T(8,128)(2,1)S(1)} collective-permute-done((bf16[320,4,1,128]{3,0,2,1:T(8,128)(2,1)S(1)}, bf16[320,4,1,128]{3,0,2,1:T(8,128)(2,1)S(1)}, u32[]{:S(2)}, u32[]{:S(2)}) %collective-permute-start.4) | collective-permute-done | bytes 327712 | tf_op jit(solution)/shard_map/ppermute | solution.py:28
  673.5 7.2 %copy.26 = bf16[2,2,2,8,4,4,128]{3,2,6,1,5,0,4:T(2,128)(2,1)} copy(bf16[2,2,2,8,4,4,128]{6,3,5,4,2,1,0:T(8,128)(2,1)S(1)} %bitcast.563) | data formatting | bytes 524288 | tf_op jit(solution)/shard_map/convert_element_type | solution.py:138
  680.7 4.4 copy.27
  (240 shorter events, 155.8 us)
Async XLA Ops:
  6.5 640.1 %copy-start = (f32[320,320]{1,0:T(8,128)S(1)}, f32[320,320]{1,0:T(8,128)}, u32[]{:S(2)}) copy-start(f32[320,320]{1,0:T(8,128)} %param.20) | copy-start | bytes 1228804
  6.5 3.3 copy-start.2
  7.6 8.0 %copy-start.3 = (bf16[1,15,224,40]{2,3,1,0:T(8,128)(2,1)S(1)}, bf16[1,15,224,40]{2,3,1,0:T(8,128)(2,1)}, u32[]{:S(2)}) copy-start(bf16[1,15,224,40]{2,3,1,0:T(8,128)(2,1)} %param.15) | copy-start | bytes 806404
  7.6 2.3 collective-permute-start.2
  7.8 7.5 %collective-permute-start.3 = (bf16[40,4,2,128]{3,0,2,1:T(8,128)(2,1)S(1)}, bf16[40,4,2,128]{3,0,2,1:T(8,128)(2,1)S(1)}, u32[]{:S(2)}, u32[]{:S(2)}) collective-permute-start(bf16[40,4,2,128]{3,0,2,1:T(8,128)(2,1)S(1)} %get-tuple-element.221), channel_id=1, source_target_pairs={{1,0},{2,1},{3,2},{4,3},{5,4},{6,5},{7,6},{8,7},{9,8},{10,9},{11,1... | collective-permute-start | bytes 245768 | tf_op jit(solution)/shard_map/ppermute | solution.py:15
  18.8 0.9 copy-start.1
  20.8 0.9 copy-start.5
  21.7 4.6 copy-start.6
  21.7 4.6 copy-start.8
  26.3 620.4 %copy-start.7 = (f32[320]{0:T(512)S(1)}, f32[320]{0:T(512)}, u32[]{:S(2)}) copy-start(f32[320]{0:T(512)} %param.19) | copy-start | bytes 3844
  26.3 43.0 %all-gather.5.cloned.1.call-start = ((), (), s32[]{:S(2)}) async-start(), calls=%async_computation | async-start | bytes 1474560 | tf_op jit(solution)/shard_map/while/body/eval_jaxpr/all_gather | solution.py:22
  70.8 10.1 %collective-permute-start = (bf16[40,4,2,128]{3,0,2,1:T(8,128)(2,1)S(1)}, bf16[40,4,2,128]{3,0,2,1:T(8,128)(2,1)S(1)}, u32[]{:S(2)}, u32[]{:S(2)}) collective-permute-start(bf16[40,4,2,128]{3,0,2,1:T(8,128)(2,1)S(1)} %get-tuple-element.267), channel_id=1, source_target_pairs={{1,0},{2,1},{3,2},{4,3},{5,4},{6,5},{7,6},{8,7},{9,8},{10,9},{11,1... | collective-permute-start | bytes 245768 | tf_op jit(solution)/shard_map/while/body/eval_jaxpr/ppermute | solution.py:15
  77.2 3.8 collective-permute-start.1
  102.8 44.2 %all-gather.5.cloned.1.call-start = ((), (), s32[]{:S(2)}) async-start(), calls=%async_computation | async-start | bytes 1474560 | tf_op jit(solution)/shard_map/while/body/eval_jaxpr/all_gather | solution.py:22
  148.5 10.1 %collective-permute-start = (bf16[40,4,2,128]{3,0,2,1:T(8,128)(2,1)S(1)}, bf16[40,4,2,128]{3,0,2,1:T(8,128)(2,1)S(1)}, u32[]{:S(2)}, u32[]{:S(2)}) collective-permute-start(bf16[40,4,2,128]{3,0,2,1:T(8,128)(2,1)S(1)} %get-tuple-element.267), channel_id=1, source_target_pairs={{1,0},{2,1},{3,2},{4,3},{5,4},{6,5},{7,6},{8,7},{9,8},{10,9},{11,1... | collective-permute-start | bytes 245768 | tf_op jit(solution)/shard_map/while/body/eval_jaxpr/ppermute | solution.py:15
  154.9 3.8 collective-permute-start.1
  180.5 44.2 %all-gather.5.cloned.1.call-start = ((), (), s32[]{:S(2)}) async-start(), calls=%async_computation | async-start | bytes 1474560 | tf_op jit(solution)/shard_map/while/body/eval_jaxpr/all_gather | solution.py:22
  226.2 10.1 %collective-permute-start = (bf16[40,4,2,128]{3,0,2,1:T(8,128)(2,1)S(1)}, bf16[40,4,2,128]{3,0,2,1:T(8,128)(2,1)S(1)}, u32[]{:S(2)}, u32[]{:S(2)}) collective-permute-start(bf16[40,4,2,128]{3,0,2,1:T(8,128)(2,1)S(1)} %get-tuple-element.267), channel_id=1, source_target_pairs={{1,0},{2,1},{3,2},{4,3},{5,4},{6,5},{7,6},{8,7},{9,8},{10,9},{11,1... | collective-permute-start | bytes 245768 | tf_op jit(solution)/shard_map/while/body/eval_jaxpr/ppermute | solution.py:15
  232.6 3.8 collective-permute-start.1
  258.2 44.2 %all-gather.5.cloned.1.call-start = ((), (), s32[]{:S(2)}) async-start(), calls=%async_computation | async-start | bytes 1474560 | tf_op jit(solution)/shard_map/while/body/eval_jaxpr/all_gather | solution.py:22
  303.9 10.1 %collective-permute-start = (bf16[40,4,2,128]{3,0,2,1:T(8,128)(2,1)S(1)}, bf16[40,4,2,128]{3,0,2,1:T(8,128)(2,1)S(1)}, u32[]{:S(2)}, u32[]{:S(2)}) collective-permute-start(bf16[40,4,2,128]{3,0,2,1:T(8,128)(2,1)S(1)} %get-tuple-element.267), channel_id=1, source_target_pairs={{1,0},{2,1},{3,2},{4,3},{5,4},{6,5},{7,6},{8,7},{9,8},{10,9},{11,1... | collective-permute-start | bytes 245768 | tf_op jit(solution)/shard_map/while/body/eval_jaxpr/ppermute | solution.py:15
  310.3 3.8 collective-permute-start.1
  335.9 44.2 %all-gather.5.cloned.1.call-start = ((), (), s32[]{:S(2)}) async-start(), calls=%async_computation | async-start | bytes 1474560 | tf_op jit(solution)/shard_map/while/body/eval_jaxpr/all_gather | solution.py:22
  381.6 10.1 %collective-permute-start = (bf16[40,4,2,128]{3,0,2,1:T(8,128)(2,1)S(1)}, bf16[40,4,2,128]{3,0,2,1:T(8,128)(2,1)S(1)}, u32[]{:S(2)}, u32[]{:S(2)}) collective-permute-start(bf16[40,4,2,128]{3,0,2,1:T(8,128)(2,1)S(1)} %get-tuple-element.267), channel_id=1, source_target_pairs={{1,0},{2,1},{3,2},{4,3},{5,4},{6,5},{7,6},{8,7},{9,8},{10,9},{11,1... | collective-permute-start | bytes 245768 | tf_op jit(solution)/shard_map/while/body/eval_jaxpr/ppermute | solution.py:15
  388.0 3.8 collective-permute-start.1
  413.6 44.2 %all-gather.5.cloned.1.call-start = ((), (), s32[]{:S(2)}) async-start(), calls=%async_computation | async-start | bytes 1474560 | tf_op jit(solution)/shard_map/while/body/eval_jaxpr/all_gather | solution.py:22
  459.3 10.1 %collective-permute-start = (bf16[40,4,2,128]{3,0,2,1:T(8,128)(2,1)S(1)}, bf16[40,4,2,128]{3,0,2,1:T(8,128)(2,1)S(1)}, u32[]{:S(2)}, u32[]{:S(2)}) collective-permute-start(bf16[40,4,2,128]{3,0,2,1:T(8,128)(2,1)S(1)} %get-tuple-element.267), channel_id=1, source_target_pairs={{1,0},{2,1},{3,2},{4,3},{5,4},{6,5},{7,6},{8,7},{9,8},{10,9},{11,1... | collective-permute-start | bytes 245768 | tf_op jit(solution)/shard_map/while/body/eval_jaxpr/ppermute | solution.py:15
  465.7 3.8 collective-permute-start.1
  491.3 44.2 %all-gather.5.cloned.1.call-start = ((), (), s32[]{:S(2)}) async-start(), calls=%async_computation | async-start | bytes 1474560 | tf_op jit(solution)/shard_map/while/body/eval_jaxpr/all_gather | solution.py:22
  537.0 10.1 %collective-permute-start = (bf16[40,4,2,128]{3,0,2,1:T(8,128)(2,1)S(1)}, bf16[40,4,2,128]{3,0,2,1:T(8,128)(2,1)S(1)}, u32[]{:S(2)}, u32[]{:S(2)}) collective-permute-start(bf16[40,4,2,128]{3,0,2,1:T(8,128)(2,1)S(1)} %get-tuple-element.267), channel_id=1, source_target_pairs={{1,0},{2,1},{3,2},{4,3},{5,4},{6,5},{7,6},{8,7},{9,8},{10,9},{11,1... | collective-permute-start | bytes 245768 | tf_op jit(solution)/shard_map/while/body/eval_jaxpr/ppermute | solution.py:15
  543.4 3.8 collective-permute-start.1
  569.0 44.2 %all-gather.5.cloned.1.call-start = ((), (), s32[]{:S(2)}) async-start(), calls=%async_computation | async-start | bytes 1474560 | tf_op jit(solution)/shard_map/while/body/eval_jaxpr/all_gather | solution.py:22
  614.7 10.1 %collective-permute-start = (bf16[40,4,2,128]{3,0,2,1:T(8,128)(2,1)S(1)}, bf16[40,4,2,128]{3,0,2,1:T(8,128)(2,1)S(1)}, u32[]{:S(2)}, u32[]{:S(2)}) collective-permute-start(bf16[40,4,2,128]{3,0,2,1:T(8,128)(2,1)S(1)} %get-tuple-element.267), channel_id=1, source_target_pairs={{1,0},{2,1},{3,2},{4,3},{5,4},{6,5},{7,6},{8,7},{9,8},{10,9},{11,1... | collective-permute-start | bytes 245768 | tf_op jit(solution)/shard_map/while/body/eval_jaxpr/ppermute | solution.py:15
  621.1 3.8 collective-permute-start.1
  646.7 7.1 %copy-start.4 = (bf16[27,8,320]{2,1,0:T(8,128)(2,1)S(1)}, bf16[27,8,320]{2,1,0:T(8,128)(2,1)}, u32[]{:S(2)}) copy-start(bf16[27,8,320]{2,1,0:T(8,128)(2,1)} %param.21) | copy-start | bytes 414724
  655.6 10.5 %collective-permute-start.4 = (bf16[320,4,1,128]{3,0,2,1:T(8,128)(2,1)S(1)}, bf16[320,4,1,128]{3,0,2,1:T(8,128)(2,1)S(1)}, u32[]{:S(2)}, u32[]{:S(2)}) collective-permute-start(bf16[320,4,1,128]{3,0,2,1:T(8,128)(2,1)S(1)} %slice.707), channel_id=1, source_target_pairs={{0,31},{1,0},{2,1},{3,2},{4,3},{5,4},{6,5},{7,6},{8,7},{9,8},{10,9... | collective-permute-start | bytes 983048 | tf_op jit(solution)/shard_map/ppermute | solution.py:28
Sparse Core Ops, SparseCore 0:
  34.0 35.2 all-gather.4
  110.5 36.4 all-gather.4
  188.2 36.4 all-gather.4
  265.9 36.4 all-gather.4
  343.6 36.4 all-gather.4
  421.3 36.4 all-gather.4
  499.0 36.4 all-gather.4
  576.7 36.4 all-gather.4
